TPU v7x, 32 devices: a whole 2x2x4 slice. The times are simulated.
32 devices in a mesh: runs: 2 (over y), ja: 16 (over z, x, core).
Axes of the slice: x: 2, y: 2, z: 4, core: 2. Of those that a mesh axis runs over, the one named last changes fastest.
Arguments:
- pos_vel: float32 [6, 32768], P(None, ('runs', 'ja')), parts along dimension 1, may hold values from -4 to 4
- acc_jerk: float32 [6, 32768], P(None, ('runs', 'ja')), parts along dimension 1, may hold values from -5 to 5
- star_mass: float32 [32768], P(('runs', 'ja')), parts along dimension 0, may hold values from 1.2207031e-05 to 0.00030517578
- step_phase: float32 [32768], P(('runs', 'ja')), parts along dimension 0, may hold values from 0.25 to 1
- step_level: int32 [32768], P(('runs', 'ja')), parts along dimension 0, may hold values from 0 to 3
- counts: int32 [32], P(('runs', 'ja')), parts along dimension 0, may hold values from 1 to 256, 2048 in all
- star_order: int32 [32, 1024], P(('runs', 'ja')), parts along dimension 0, may hold values from 0 to 1023, each once within a row
Outputs:
- new_pos_vel: float32 [6, 32768], P(None, ('runs', 'ja')), parts along dimension 1
- new_acc_jerk: float32 [6, 32768], P(None, ('runs', 'ja')), parts along dimension 1
- active_state: float32 [12, 8192], P(None, ('runs', 'ja')), parts along dimension 1
There are 2 independent parts, one for each index of `runs`. A program takes and returns all parts, laid end to end along the dimension named above; each array names one. Nothing has to cross between parts.
Inputs may be any that keep to these rules, and one draw needn't show every extreme that they name: The counts sum to 2048; the largest is exactly 256. `star_order`: each row is a permutation of the local indices.
All inputs are finite; a program needn't handle non-finite values. No bound on the sum of `counts` on one device may be relied on, other than what follows from the above.
Results may differ from a plain program's by a relative error of at most 0.00002.
Values sent between devices are 32-bit elements; how exact they have to be, the bound alone decides.
A program may use at most 64 MiB of HBM per device.

v0:
```python
import math
import jax
import jax.numpy as jnp
from jax import lax
from jax.sharding import PartitionSpec as P

A_DEV = 128
soft_sq = 0.01
base_step = 2.0


def predict(pos_vel, acc_jerk, age):
    half_sq = 0.5 * age * age
    sixth_cube = age * age * age / 6.0
    position = (
        pos_vel[0:3] + age * pos_vel[3:6] + half_sq * acc_jerk[0:3] + sixth_cube * acc_jerk[3:6]
    )
    velocity = pos_vel[3:6] + age * acc_jerk[0:3] + half_sq * acc_jerk[3:6]
    return jnp.concatenate([position, velocity], axis=0)


def pair_block(targets, sources):
    delta_x = sources[0:3, None, :] - targets[0:3, :, None]
    delta_v = sources[3:6, None, :] - targets[3:6, :, None]
    dist_sq = soft_sq + delta_x[0] * delta_x[0] + delta_x[1] * delta_x[1] + delta_x[2] * delta_x[2]
    inverse = lax.rsqrt(dist_sq)
    inverse_sq = inverse * inverse
    weight = sources[6][None, :] * inverse * inverse_sq
    radial = (
        3.0
        * (delta_x[0] * delta_v[0] + delta_x[1] * delta_v[1] + delta_x[2] * delta_v[2])
        * inverse_sq
    )
    accel_part = jnp.sum(weight[None] * delta_x, axis=2)
    jerk_part = jnp.sum(weight[None] * (delta_v - radial[None] * delta_x), axis=2)
    return jnp.concatenate([accel_part, jerk_part], axis=0)


def pair_forces(targets, sources):
    rows = targets.shape[1]
    block = math.gcd(rows, 512)
    split = targets.reshape(6, rows // block, block).transpose(1, 0, 2)
    result = lax.map(lambda part: pair_block(part, sources), split)
    return result.transpose(1, 0, 2).reshape(6, rows)


def correct(old_pv, old_aj, fresh, step_len):
    half = 0.5 * step_len
    twelfth = step_len * step_len / 12.0
    velocity = (
        old_pv[3:6] + half * (old_aj[0:3] + fresh[0:3]) + twelfth * (old_aj[3:6] - fresh[3:6])
    )
    position = old_pv[0:3] + half * (old_pv[3:6] + velocity) + twelfth * (old_aj[0:3] - fresh[0:3])
    return jnp.concatenate([position, velocity], axis=0)


def per_device(pos_vel, acc_jerk, star_mass, step_phase, step_level, counts, star_order):
    capacity = 2 * A_DEV
    per_owner = pos_vel.shape[1]
    slot_ids = star_order[0, :capacity]
    live = jnp.arange(capacity, dtype=jnp.int32) < counts[0]
    step_len = base_step * jnp.exp2(-step_level.astype(jnp.float32))
    is_active = jnp.zeros((per_owner,), jnp.float32).at[slot_ids].set(live.astype(jnp.float32))
    age = step_len * jnp.where(is_active > 0.5, jnp.float32(1.0), step_phase)
    predicted = predict(pos_vel, acc_jerk, age)
    sources = jnp.concatenate([predicted, star_mass[None, :]], axis=0)
    targets = predicted[:, slot_ids]
    every_slot = pair_forces(lax.all_gather(targets, "ja", axis=1, tiled=True), sources)
    fresh = lax.psum_scatter(every_slot, "ja", scatter_dimension=1, tiled=True)
    old_pv = pos_vel[:, slot_ids]
    old_aj = acc_jerk[:, slot_ids]
    corrected = correct(old_pv, old_aj, fresh, step_len[slot_ids])
    kept_pv = jnp.where(live[None, :], corrected, old_pv)
    kept_aj = jnp.where(live[None, :], fresh, old_aj)
    fresh_state = jnp.concatenate([corrected, fresh], axis=0)
    active_state = jnp.where(live[None, :], fresh_state, jnp.zeros_like(fresh_state))
    return (
        pos_vel.at[:, slot_ids].set(kept_pv),
        acc_jerk.at[:, slot_ids].set(kept_aj),
        active_state,
    )


def solution(mesh):
    in_specs = (
        P(None, ("runs", "ja")),
        P(None, ("runs", "ja")),
        P(("runs", "ja")),
        P(("runs", "ja")),
        P(("runs", "ja")),
        P(("runs", "ja")),
        P(("runs", "ja"), None),
    )
    out_specs = (P(None, ("runs", "ja")), P(None, ("runs", "ja")), P(None, ("runs", "ja")))
    return jax.shard_map(
        per_device, mesh=mesh, in_specs=in_specs, out_specs=out_specs, check_vma=False
    )
```

profile of v0, /device:TPU:0, one launch (start us, length us, event | category | flops | bytes accessed | tf_op | source)
XLA Modules:
  0.0 163.4 jit_solution(9039283092665602739)
XLA Ops:
  8.6 1.4 scatter_custom_fusion
  12.6 32.3 %all-gather = f32[6,4096]{0,1:T(8,128)S(1)} all-gather(f32[6,256]{0,1:T(8,128)S(1)} %bitcast.44), channel_id=2, replica_groups=mesh['runs'=2,'ja'=16] {'ja'}, dimensions={1}, use_global_device_ids=true | all-gather | bytes 104448 | tf_op jit(solution)/shard_map/all_gather | solution.py:68
  45.5 45.8 %while.10 = (s32[]{:T(128)}, f32[8,6,512]{2,1,0:T(8,128)S(1)}, f32[1,1024]{1,0:T(1,128)S(1)}, f32[3,1024]{1,0:T(4,128)S(1)}, f32[8,6,512]{2,1,0:T(8,128)S(1)}, /...) while((s32[]{:T(128)}, f32[8,6,512]{2,1,0:T(8,128)S(1)}, f32[1,1024]{1,0:T(1,128)S(1)}, ...), condition=%wide.region_4.5_spmd, body=%wide.region_1.4_spmd.sunk | while | flops 24117252 | bytes 33702004 | solution.py:43
  46.6 2.1 %fusion.17 = (f32[512,1024]{1,0:T(8,128)S(1)}, f32[512,1024]{1,0:T(8,128)S(1)}) fusion(f32[3,512,1024]{2,1,0:T(8,128)S(1)} %get-tuple-element.141, f32[3,512,1024]{2,1,0:T(8,128)S(1)} %get-tuple-element.142, f32[1024]{0:T(1024)S(1)} %bitcast.47), kind=kLoop, calls=%fused_computation.15.clone.1 | loop fusion | flops 8388608 | bytes 16781312 | tf_op jit(solution)/shard_map/while/body/eval_jaxpr/mul | solution.py:35
  48.7 2.5 %multiply_reduce_fusion.3 = (f32[3,512]{1,0:T(4,128)S(1)}, f32[3,512]{1,0:T(4,128)S(1)}) fusion(f32[512,1024]{1,0:T(8,128)S(1)} %get-tuple-element.143, f32[3,512]{1,0:T(4,128)S(1)} %get-tuple-element.140, f32[3,1024]{1,0:T(4,128)S(1)} %get-tuple-element.168, f32[512,1024]{1,0:T(8,128)S(1)} %get-tuple-element.144, ...), kind=kLoop, calls=%fused_computation.8.clone.1 | loop fusion | flops 12579840 | bytes 4243456 | tf_op jit(solution)/shard_map/while/body/eval_jaxpr/reduce_sum | solution.py:34
  52.3 2.1 %fusion.17 = (f32[512,1024]{1,0:T(8,128)S(1)}, f32[512,1024]{1,0:T(8,128)S(1)}) fusion(f32[3,512,1024]{2,1,0:T(8,128)S(1)} %get-tuple-element.141, f32[3,512,1024]{2,1,0:T(8,128)S(1)} %get-tuple-element.142, f32[1024]{0:T(1024)S(1)} %bitcast.47), kind=kLoop, calls=%fused_computation.15.clone.1 | loop fusion | flops 8388608 | bytes 16781312 | tf_op jit(solution)/shard_map/while/body/eval_jaxpr/mul | solution.py:35
  54.4 2.5 %multiply_reduce_fusion.3 = (f32[3,512]{1,0:T(4,128)S(1)}, f32[3,512]{1,0:T(4,128)S(1)}) fusion(f32[512,1024]{1,0:T(8,128)S(1)} %get-tuple-element.143, f32[3,512]{1,0:T(4,128)S(1)} %get-tuple-element.140, f32[3,1024]{1,0:T(4,128)S(1)} %get-tuple-element.168, f32[512,1024]{1,0:T(8,128)S(1)} %get-tuple-element.144, ...), kind=kLoop, calls=%fused_computation.8.clone.1 | loop fusion | flops 12579840 | bytes 4243456 | tf_op jit(solution)/shard_map/while/body/eval_jaxpr/reduce_sum | solution.py:34
  58.0 2.1 %fusion.17 = (f32[512,1024]{1,0:T(8,128)S(1)}, f32[512,1024]{1,0:T(8,128)S(1)}) fusion(f32[3,512,1024]{2,1,0:T(8,128)S(1)} %get-tuple-element.141, f32[3,512,1024]{2,1,0:T(8,128)S(1)} %get-tuple-element.142, f32[1024]{0:T(1024)S(1)} %bitcast.47), kind=kLoop, calls=%fused_computation.15.clone.1 | loop fusion | flops 8388608 | bytes 16781312 | tf_op jit(solution)/shard_map/while/body/eval_jaxpr/mul | solution.py:35
  60.1 2.5 %multiply_reduce_fusion.3 = (f32[3,512]{1,0:T(4,128)S(1)}, f32[3,512]{1,0:T(4,128)S(1)}) fusion(f32[512,1024]{1,0:T(8,128)S(1)} %get-tuple-element.143, f32[3,512]{1,0:T(4,128)S(1)} %get-tuple-element.140, f32[3,1024]{1,0:T(4,128)S(1)} %get-tuple-element.168, f32[512,1024]{1,0:T(8,128)S(1)} %get-tuple-element.144, ...), kind=kLoop, calls=%fused_computation.8.clone.1 | loop fusion | flops 12579840 | bytes 4243456 | tf_op jit(solution)/shard_map/while/body/eval_jaxpr/reduce_sum | solution.py:34
  63.8 2.1 %fusion.17 = (f32[512,1024]{1,0:T(8,128)S(1)}, f32[512,1024]{1,0:T(8,128)S(1)}) fusion(f32[3,512,1024]{2,1,0:T(8,128)S(1)} %get-tuple-element.141, f32[3,512,1024]{2,1,0:T(8,128)S(1)} %get-tuple-element.142, f32[1024]{0:T(1024)S(1)} %bitcast.47), kind=kLoop, calls=%fused_computation.15.clone.1 | loop fusion | flops 8388608 | bytes 16781312 | tf_op jit(solution)/shard_map/while/body/eval_jaxpr/mul | solution.py:35
  65.8 2.5 %multiply_reduce_fusion.3 = (f32[3,512]{1,0:T(4,128)S(1)}, f32[3,512]{1,0:T(4,128)S(1)}) fusion(f32[512,1024]{1,0:T(8,128)S(1)} %get-tuple-element.143, f32[3,512]{1,0:T(4,128)S(1)} %get-tuple-element.140, f32[3,1024]{1,0:T(4,128)S(1)} %get-tuple-element.168, f32[512,1024]{1,0:T(8,128)S(1)} %get-tuple-element.144, ...), kind=kLoop, calls=%fused_computation.8.clone.1 | loop fusion | flops 12579840 | bytes 4243456 | tf_op jit(solution)/shard_map/while/body/eval_jaxpr/reduce_sum | solution.py:34
  69.5 2.1 %fusion.17 = (f32[512,1024]{1,0:T(8,128)S(1)}, f32[512,1024]{1,0:T(8,128)S(1)}) fusion(f32[3,512,1024]{2,1,0:T(8,128)S(1)} %get-tuple-element.141, f32[3,512,1024]{2,1,0:T(8,128)S(1)} %get-tuple-element.142, f32[1024]{0:T(1024)S(1)} %bitcast.47), kind=kLoop, calls=%fused_computation.15.clone.1 | loop fusion | flops 8388608 | bytes 16781312 | tf_op jit(solution)/shard_map/while/body/eval_jaxpr/mul | solution.py:35
  71.6 2.5 %multiply_reduce_fusion.3 = (f32[3,512]{1,0:T(4,128)S(1)}, f32[3,512]{1,0:T(4,128)S(1)}) fusion(f32[512,1024]{1,0:T(8,128)S(1)} %get-tuple-element.143, f32[3,512]{1,0:T(4,128)S(1)} %get-tuple-element.140, f32[3,1024]{1,0:T(4,128)S(1)} %get-tuple-element.168, f32[512,1024]{1,0:T(8,128)S(1)} %get-tuple-element.144, ...), kind=kLoop, calls=%fused_computation.8.clone.1 | loop fusion | flops 12579840 | bytes 4243456 | tf_op jit(solution)/shard_map/while/body/eval_jaxpr/reduce_sum | solution.py:34
  75.2 2.1 %fusion.17 = (f32[512,1024]{1,0:T(8,128)S(1)}, f32[512,1024]{1,0:T(8,128)S(1)}) fusion(f32[3,512,1024]{2,1,0:T(8,128)S(1)} %get-tuple-element.141, f32[3,512,1024]{2,1,0:T(8,128)S(1)} %get-tuple-element.142, f32[1024]{0:T(1024)S(1)} %bitcast.47), kind=kLoop, calls=%fused_computation.15.clone.1 | loop fusion | flops 8388608 | bytes 16781312 | tf_op jit(solution)/shard_map/while/body/eval_jaxpr/mul | solution.py:35
  77.3 2.5 %multiply_reduce_fusion.3 = (f32[3,512]{1,0:T(4,128)S(1)}, f32[3,512]{1,0:T(4,128)S(1)}) fusion(f32[512,1024]{1,0:T(8,128)S(1)} %get-tuple-element.143, f32[3,512]{1,0:T(4,128)S(1)} %get-tuple-element.140, f32[3,1024]{1,0:T(4,128)S(1)} %get-tuple-element.168, f32[512,1024]{1,0:T(8,128)S(1)} %get-tuple-element.144, ...), kind=kLoop, calls=%fused_computation.8.clone.1 | loop fusion | flops 12579840 | bytes 4243456 | tf_op jit(solution)/shard_map/while/body/eval_jaxpr/reduce_sum | solution.py:34
  80.9 2.1 %fusion.17 = (f32[512,1024]{1,0:T(8,128)S(1)}, f32[512,1024]{1,0:T(8,128)S(1)}) fusion(f32[3,512,1024]{2,1,0:T(8,128)S(1)} %get-tuple-element.141, f32[3,512,1024]{2,1,0:T(8,128)S(1)} %get-tuple-element.142, f32[1024]{0:T(1024)S(1)} %bitcast.47), kind=kLoop, calls=%fused_computation.15.clone.1 | loop fusion | flops 8388608 | bytes 16781312 | tf_op jit(solution)/shard_map/while/body/eval_jaxpr/mul | solution.py:35
  83.0 2.5 %multiply_reduce_fusion.3 = (f32[3,512]{1,0:T(4,128)S(1)}, f32[3,512]{1,0:T(4,128)S(1)}) fusion(f32[512,1024]{1,0:T(8,128)S(1)} %get-tuple-element.143, f32[3,512]{1,0:T(4,128)S(1)} %get-tuple-element.140, f32[3,1024]{1,0:T(4,128)S(1)} %get-tuple-element.168, f32[512,1024]{1,0:T(8,128)S(1)} %get-tuple-element.144, ...), kind=kLoop, calls=%fused_computation.8.clone.1 | loop fusion | flops 12579840 | bytes 4243456 | tf_op jit(solution)/shard_map/while/body/eval_jaxpr/reduce_sum | solution.py:34
  86.6 2.1 %fusion.17 = (f32[512,1024]{1,0:T(8,128)S(1)}, f32[512,1024]{1,0:T(8,128)S(1)}) fusion(f32[3,512,1024]{2,1,0:T(8,128)S(1)} %get-tuple-element.141, f32[3,512,1024]{2,1,0:T(8,128)S(1)} %get-tuple-element.142, f32[1024]{0:T(1024)S(1)} %bitcast.47), kind=kLoop, calls=%fused_computation.15.clone.1 | loop fusion | flops 8388608 | bytes 16781312 | tf_op jit(solution)/shard_map/while/body/eval_jaxpr/mul | solution.py:35
  88.7 2.5 %multiply_reduce_fusion.3 = (f32[3,512]{1,0:T(4,128)S(1)}, f32[3,512]{1,0:T(4,128)S(1)}) fusion(f32[512,1024]{1,0:T(8,128)S(1)} %get-tuple-element.143, f32[3,512]{1,0:T(4,128)S(1)} %get-tuple-element.140, f32[3,1024]{1,0:T(4,128)S(1)} %get-tuple-element.168, f32[512,1024]{1,0:T(8,128)S(1)} %get-tuple-element.144, ...), kind=kLoop, calls=%fused_computation.8.clone.1 | loop fusion | flops 12579840 | bytes 4243456 | tf_op jit(solution)/shard_map/while/body/eval_jaxpr/reduce_sum | solution.py:34
  91.9 1.4 gather_fusion.1
  95.4 53.7 %reduce-scatter.2.cloned.1.call-done = f32[6,256]{1,0:T(8,128)} async-done(((f32[6,4096]{1,0:T(8,128)}), f32[6,256]{1,0:T(8,128)}) %reduce-scatter.2.cloned.1.call-update) | async-done | bytes 6160 | tf_op jit(solution)/shard_map/reduce_scatter | solution.py:69
  150.7 1.4 scatter_fusion.1
  153.0 1.4 scatter_fusion
  155.2 1.3 maximum_select_fusion
  (59 shorter events, 18.7 us)
Async XLA Ops:
  7.2 141.9 %reduce-scatter.2.cloned.1.call-start = ((), (), s32[]{:S(2)}) async-start(), calls=%async_computation.1 | async-start | bytes 139264 | tf_op jit(solution)/shard_map/reduce_scatter | solution.py:69
  12.6 32.9 %copy-start.3 = (f32[1024]{0:T(1024)S(1)}, f32[1024]{0:T(1024)}, u32[]{:S(2)}) copy-start(f32[1024]{0:T(1024)} %param.11) | copy-start | bytes 12292
  45.5 47.8 %copy-start = (f32[6,1024]{1,0:T(8,128)S(1)}, f32[6,1024]{1,0:T(8,128)}, u32[]{:S(2)}) copy-start(f32[6,1024]{1,0:T(8,128)} %param.10) | copy-start | bytes 73732
  45.5 48.1 %copy-start.1 = (f32[6,1024]{1,0:T(8,128)S(1)}, f32[6,1024]{1,0:T(8,128)}, u32[]{:S(2)}) copy-start(f32[6,1024]{1,0:T(8,128)} %param.9) | copy-start | bytes 73732
  91.2 0.6 copy-start.2
Sparse Core Ops, SparseCore 0:
  92.0 56.9 reduce-scatter.1
where the time goes:
time: 164 us; the launch traced here: 163 us
  waiting for transfers between devices  53.7 us (33%)
  other arithmetic  50.4 us (31%)
  blocking collectives  32.3 us (20%)
  between operations  14.8 us (9%)
  local copies, waits for them, and re-layouts  11.8 us (7%)
    reduce_scatter x1, waiting for transfers between devices, per_device(): fresh = lax.psum_scatter(every_slot, 'ja', scatter_dimension=1, tiled=True)  53.7 us
    all_gather x1, blocking collectives, per_device(): lax.all_gather(targets, 'ja', axis=1, tiled=True)  32.3 us
    reduce_sum x8, other arithmetic, pair_block(): accel_part = jnp.sum(weight[None] * delta_x, axis=2)  20 us
    mul x8, other arithmetic, pair_block(): radial[None] * delta_x  16.6 us
    sub x8, other arithmetic, pair_block(): delta_v = sources[3:6, None, :] - targets[3:6, :, None]  8.53 us
  transfers between devices with their start and end apart: 1, of which 1 were waited for; matrix products, arithmetic and copies ran while one was open for 2% of the time, Pallas kernels for 0%

commit v1 on v0

--- a/solution.py
+++ b/solution.py
@@ -1,3 +1,4 @@
+import functools
 import math
 import jax
 import jax.numpy as jnp
@@ -7,6 +8,35 @@
 A_DEV = 128
 soft_sq = 0.01
 base_step = 2.0
+
+
+def _derive_terms(body, pos_dim):
+    back = list(body.shape[1:])
+    back[pos_dim] *= body.shape[0]
+    return jnp.moveaxis(body, 0, pos_dim).reshape(back)
+
+
+def solve_the_trees(array_here, mesh_name, k_dim):
+    size_here = lax.axis_size(mesh_name)
+    fields = [(c, (c + 1) % size_here) for c in range(size_here)]
+    buffers = [(w, k0) for k0, w in fields]
+    w1, right_arr = ([], [])
+    for it in range(size_here - 1):
+        if it % 2 == 0:
+            outcome_arr = lax.ppermute(w1[-1] if w1 else array_here, mesh_name, fields)
+            w1.append(outcome_arr)
+        else:
+            right_arr.append(
+                lax.ppermute(right_arr[-1] if right_arr else array_here, mesh_name, buffers)
+            )
+    after = jnp.stack([*w1[::-1], array_here, *right_arr])
+    b_next = lax.axis_index(mesh_name)
+    finding = b_next - len(w1)
+    after = after[(jnp.arange(size_here) - finding) % size_here]
+    return _derive_terms(after, k_dim)
+
+
+_spread_ports = functools.partial(solve_the_trees, mesh_name="ja", k_dim=1)
 
 
 def predict(pos_vel, acc_jerk, age):
@@ -65,7 +95,7 @@
     predicted = predict(pos_vel, acc_jerk, age)
     sources = jnp.concatenate([predicted, star_mass[None, :]], axis=0)
     targets = predicted[:, slot_ids]
-    every_slot = pair_forces(lax.all_gather(targets, "ja", axis=1, tiled=True), sources)
+    every_slot = pair_forces(_spread_ports(targets), sources)
     fresh = lax.psum_scatter(every_slot, "ja", scatter_dimension=1, tiled=True)
     old_pv = pos_vel[:, slot_ids]
     old_aj = acc_jerk[:, slot_ids]

time: 164 us -> 192 us (1.17)
  blocking collectives: 32.3 us -> 0 us
  starting transfers between devices: 0.04 us -> 31.9 us
  waiting for transfers between devices: 53.7 us -> 78.1 us
  local copies, waits for them, and re-layouts: 11.8 us -> 16.2 us
    all_gather x1 -> x0, blocking collectives: 32.3 us -> none  [per_device(): lax.all_gather(targets, 'ja', axis=1, tiled=True)]
    ppermute x0 -> x15, starting transfers between devices: none -> 31.8 us  [the longest x7 31.3 us: solve_the_trees(): lax.ppermute(right_arr[-1] if right_arr else array_here, mesh_name, buffers)]
    ppermute x0 -> x15, waiting for transfers between devices: none -> 25.1 us  [the longest x8 25.1 us: solve_the_trees(): outcome_arr = lax.ppermute(w1[-1] if w1 else array_here, mesh_name, fields)]
    unnamed x12 -> x37, local copies, waits for them, and re-layouts: 2.7 us -> 6.55 us
  transfers between devices with their start and end apart: 1 -> 16, of which waited for: 1 -> 9; matrix products, arithmetic and copies ran while one was open for 2% -> 4% of each run, Pallas kernels for 0% -> 0%
where the time goes in v1:
time: 192 us; the launch traced here: 191 us
  waiting for transfers between devices  78.1 us (41%)
  other arithmetic  49.9 us (26%)
  starting transfers between devices  31.9 us (17%)
  local copies, waits for them, and re-layouts  16.2 us (8%)
  between operations  15.1 us (8%)
    reduce_scatter x1, waiting for transfers between devices, per_device(): fresh = lax.psum_scatter(every_slot, 'ja', scatter_dimension=1, tiled=True)  52.9 us
    ppermute x7, starting transfers between devices, solve_the_trees(): lax.ppermute(right_arr[-1] if right_arr else array_here, mesh_name, buffers)  31.3 us
    ppermute x8, waiting for transfers between devices, solve_the_trees(): outcome_arr = lax.ppermute(w1[-1] if w1 else array_here, mesh_name, fields)  25.1 us
    reduce_sum x8, other arithmetic, pair_block(): accel_part = jnp.sum(weight[None] * delta_x, axis=2)  19.5 us
    mul x8, other arithmetic, pair_block(): radial[None] * delta_x  16.6 us
    sub x8, other arithmetic, pair_block(): delta_v = sources[3:6, None, :] - targets[3:6, :, None]  8.53 us
    unnamed x37, local copies, waits for them, and re-layouts  6.55 us
  transfers between devices with their start and end apart: 16, of which 9 were waited for; matrix products, arithmetic and copies ran while one was open for 4% of the time, Pallas kernels for 0%

profile of v1, /device:TPU:0, one launch (start us, length us, event | category | flops | bytes accessed | tf_op | source)
XLA Modules:
  0.0 191.5 jit_solution(10558629846780840214)
XLA Ops:
  13.1 7.6 %collective-permute-done = f32[6,256]{0,1:T(8,128)S(1)} collective-permute-done((f32[6,256]{0,1:T(8,128)S(1)}, f32[6,256]{0,1:T(8,128)S(1)}, u32[]{:S(2)}, u32[]{:S(2)}) %collective-permute-start) | collective-permute-done | bytes 6176 | tf_op jit(solution)/shard_map/ppermute | solution.py:26
  20.7 4.4 %collective-permute-start.8 = (f32[6,256]{0,1:T(8,128)S(1)}, f32[6,256]{0,1:T(8,128)S(1)}, u32[]{:S(2)}, u32[]{:S(2)}) collective-permute-start(f32[6,256]{0,1:T(8,128)S(1)} %bitcast.82), channel_id=1, source_target_pairs={{1,0},{2,1},{3,2},{4,3},{5,4},{6,5},{7,6},{8,7},{9,8},{10,9},{11,1... | collective-permute-start | bytes 18440 | tf_op jit(solution)/shard_map/ppermute | solution.py:30
  25.1 2.7 %collective-permute-done.1 = f32[6,256]{0,1:T(8,128)S(1)} collective-permute-done((f32[6,256]{0,1:T(8,128)S(1)}, f32[6,256]{0,1:T(8,128)S(1)}, u32[]{:S(2)}, u32[]{:S(2)}) %collective-permute-start.1) | collective-permute-done | bytes 6176 | tf_op jit(solution)/shard_map/ppermute | solution.py:26
  27.8 4.5 %collective-permute-start.9 = (f32[6,256]{0,1:T(8,128)S(1)}, f32[6,256]{0,1:T(8,128)S(1)}, u32[]{:S(2)}, u32[]{:S(2)}) collective-permute-start(f32[6,256]{0,1:T(8,128)S(1)} %collective-permute-done.8), channel_id=1, source_target_pairs={{1,0},{2,1},{3,2},{4,3},{5,4},{6,5},{7,6},{8,7},{9,8},{10,9},{11,1... | collective-permute-start | bytes 18440 | tf_op jit(solution)/shard_map/ppermute | solution.py:30
  32.3 2.7 %collective-permute-done.2 = f32[6,256]{0,1:T(8,128)S(1)} collective-permute-done((f32[6,256]{0,1:T(8,128)S(1)}, f32[6,256]{0,1:T(8,128)S(1)}, u32[]{:S(2)}, u32[]{:S(2)}) %collective-permute-start.2) | collective-permute-done | bytes 6176 | tf_op jit(solution)/shard_map/ppermute | solution.py:26
  35.0 4.4 %collective-permute-start.10 = (f32[6,256]{0,1:T(8,128)S(1)}, f32[6,256]{0,1:T(8,128)S(1)}, u32[]{:S(2)}, u32[]{:S(2)}) collective-permute-start(f32[6,256]{0,1:T(8,128)S(1)} %collective-permute-done.9), channel_id=1, source_target_pairs={{1,0},{2,1},{3,2},{4,3},{5,4},{6,5},{7,6},{8,7},{9,8},{10,9},{11,1... | collective-permute-start | bytes 18440 | tf_op jit(solution)/shard_map/ppermute | solution.py:30
  39.4 2.7 %collective-permute-done.3 = f32[6,256]{0,1:T(8,128)S(1)} collective-permute-done((f32[6,256]{0,1:T(8,128)S(1)}, f32[6,256]{0,1:T(8,128)S(1)}, u32[]{:S(2)}, u32[]{:S(2)}) %collective-permute-start.3) | collective-permute-done | bytes 6176 | tf_op jit(solution)/shard_map/ppermute | solution.py:26
  42.2 4.4 %collective-permute-start.11 = (f32[6,256]{0,1:T(8,128)S(1)}, f32[6,256]{0,1:T(8,128)S(1)}, u32[]{:S(2)}, u32[]{:S(2)}) collective-permute-start(f32[6,256]{0,1:T(8,128)S(1)} %collective-permute-done.10), channel_id=1, source_target_pairs={{1,0},{2,1},{3,2},{4,3},{5,4},{6,5},{7,6},{8,7},{9,8},{10,9},{11,1... | collective-permute-start | bytes 18440 | tf_op jit(solution)/shard_map/ppermute | solution.py:30
  46.6 2.7 %collective-permute-done.4 = f32[6,256]{0,1:T(8,128)S(1)} collective-permute-done((f32[6,256]{0,1:T(8,128)S(1)}, f32[6,256]{0,1:T(8,128)S(1)}, u32[]{:S(2)}, u32[]{:S(2)}) %collective-permute-start.4) | collective-permute-done | bytes 6176 | tf_op jit(solution)/shard_map/ppermute | solution.py:26
  49.4 4.4 %collective-permute-start.12 = (f32[6,256]{0,1:T(8,128)S(1)}, f32[6,256]{0,1:T(8,128)S(1)}, u32[]{:S(2)}, u32[]{:S(2)}) collective-permute-start(f32[6,256]{0,1:T(8,128)S(1)} %collective-permute-done.11), channel_id=1, source_target_pairs={{1,0},{2,1},{3,2},{4,3},{5,4},{6,5},{7,6},{8,7},{9,8},{10,9},{11,1... | collective-permute-start | bytes 18440 | tf_op jit(solution)/shard_map/ppermute | solution.py:30
  53.8 2.7 %collective-permute-done.5 = f32[6,256]{0,1:T(8,128)S(1)} collective-permute-done((f32[6,256]{0,1:T(8,128)S(1)}, f32[6,256]{0,1:T(8,128)S(1)}, u32[]{:S(2)}, u32[]{:S(2)}) %collective-permute-start.5) | collective-permute-done | bytes 6176 | tf_op jit(solution)/shard_map/ppermute | solution.py:26
  56.6 4.5 %collective-permute-start.13 = (f32[6,256]{0,1:T(8,128)S(1)}, f32[6,256]{0,1:T(8,128)}, u32[]{:S(2)}, u32[]{:S(2)}) collective-permute-start(f32[6,256]{0,1:T(8,128)S(1)} %collective-permute-done.12), channel_id=1, source_target_pairs={{1,0},{2,1},{3,2},{4,3},{5,4},{6,5},{7,6},{8,7},{9,8},{10,9},{11,1... | collective-permute-start | bytes 18440 | tf_op jit(solution)/shard_map/ppermute | solution.py:30
  61.1 2.7 %collective-permute-done.6 = f32[6,256]{0,1:T(8,128)S(1)} collective-permute-done((f32[6,256]{0,1:T(8,128)S(1)}, f32[6,256]{0,1:T(8,128)S(1)}, u32[]{:S(2)}, u32[]{:S(2)}) %collective-permute-start.6) | collective-permute-done | bytes 6176 | tf_op jit(solution)/shard_map/ppermute | solution.py:26
  65.2 4.5 %collective-permute-start.14 = (f32[6,256]{0,1:T(8,128)}, f32[6,256]{0,1:T(8,128)S(1)}, u32[]{:S(2)}, u32[]{:S(2)}) collective-permute-start(f32[6,256]{0,1:T(8,128)} %collective-permute-done.13), channel_id=1, source_target_pairs={{1,0},{2,1},{3,2},{4,3},{5,4},{6,5},{7,6},{8,7},{9,8},{10,9},{11,1... | collective-permute-start | bytes 18440 | tf_op jit(solution)/shard_map/ppermute | solution.py:30
  76.2 45.2 %while.10 = (s32[]{:T(128)}, f32[8,6,512]{2,1,0:T(8,128)S(1)}, f32[1,1024]{1,0:T(1,128)S(1)}, f32[3,1024]{1,0:T(4,128)S(1)}, f32[8,6,512]{2,1,0:T(8,128)S(1)}, /...) while((s32[]{:T(128)}, f32[8,6,512]{2,1,0:T(8,128)S(1)}, f32[1,1024]{1,0:T(1,128)S(1)}, ...), condition=%wide.region_4.5_spmd, body=%wide.region_1.4_spmd.sunk | while | flops 24117252 | bytes 33702004 | solution.py:73
  79.4 2.4 %multiply_reduce_fusion.3 = (f32[3,512]{1,0:T(4,128)S(1)}, f32[3,512]{1,0:T(4,128)S(1)}) fusion(f32[512,1024]{1,0:T(8,128)S(1)} %get-tuple-element.146, f32[3,512]{1,0:T(4,128)S(1)} %get-tuple-element.143, f32[3,1024]{1,0:T(4,128)S(1)} %get-tuple-element.171, f32[512,1024]{1,0:T(8,128)S(1)} %get-tuple-element.147, ...), kind=kLoop, calls=%fused_computation.9.clone.1 | loop fusion | flops 12579840 | bytes 4243456 | tf_op jit(solution)/shard_map/while/body/eval_jaxpr/reduce_sum | solution.py:64
  85.0 2.4 %multiply_reduce_fusion.3 = (f32[3,512]{1,0:T(4,128)S(1)}, f32[3,512]{1,0:T(4,128)S(1)}) fusion(f32[512,1024]{1,0:T(8,128)S(1)} %get-tuple-element.146, f32[3,512]{1,0:T(4,128)S(1)} %get-tuple-element.143, f32[3,1024]{1,0:T(4,128)S(1)} %get-tuple-element.171, f32[512,1024]{1,0:T(8,128)S(1)} %get-tuple-element.147, ...), kind=kLoop, calls=%fused_computation.9.clone.1 | loop fusion | flops 12579840 | bytes 4243456 | tf_op jit(solution)/shard_map/while/body/eval_jaxpr/reduce_sum | solution.py:64
  90.7 2.4 %multiply_reduce_fusion.3 = (f32[3,512]{1,0:T(4,128)S(1)}, f32[3,512]{1,0:T(4,128)S(1)}) fusion(f32[512,1024]{1,0:T(8,128)S(1)} %get-tuple-element.146, f32[3,512]{1,0:T(4,128)S(1)} %get-tuple-element.143, f32[3,1024]{1,0:T(4,128)S(1)} %get-tuple-element.171, f32[512,1024]{1,0:T(8,128)S(1)} %get-tuple-element.147, ...), kind=kLoop, calls=%fused_computation.9.clone.1 | loop fusion | flops 12579840 | bytes 4243456 | tf_op jit(solution)/shard_map/while/body/eval_jaxpr/reduce_sum | solution.py:64
  96.3 2.4 %multiply_reduce_fusion.3 = (f32[3,512]{1,0:T(4,128)S(1)}, f32[3,512]{1,0:T(4,128)S(1)}) fusion(f32[512,1024]{1,0:T(8,128)S(1)} %get-tuple-element.146, f32[3,512]{1,0:T(4,128)S(1)} %get-tuple-element.143, f32[3,1024]{1,0:T(4,128)S(1)} %get-tuple-element.171, f32[512,1024]{1,0:T(8,128)S(1)} %get-tuple-element.147, ...), kind=kLoop, calls=%fused_computation.9.clone.1 | loop fusion | flops 12579840 | bytes 4243456 | tf_op jit(solution)/shard_map/while/body/eval_jaxpr/reduce_sum | solution.py:64
  102.0 2.4 %multiply_reduce_fusion.3 = (f32[3,512]{1,0:T(4,128)S(1)}, f32[3,512]{1,0:T(4,128)S(1)}) fusion(f32[512,1024]{1,0:T(8,128)S(1)} %get-tuple-element.146, f32[3,512]{1,0:T(4,128)S(1)} %get-tuple-element.143, f32[3,1024]{1,0:T(4,128)S(1)} %get-tuple-element.171, f32[512,1024]{1,0:T(8,128)S(1)} %get-tuple-element.147, ...), kind=kLoop, calls=%fused_computation.9.clone.1 | loop fusion | flops 12579840 | bytes 4243456 | tf_op jit(solution)/shard_map/while/body/eval_jaxpr/reduce_sum | solution.py:64
  107.7 2.4 %multiply_reduce_fusion.3 = (f32[3,512]{1,0:T(4,128)S(1)}, f32[3,512]{1,0:T(4,128)S(1)}) fusion(f32[512,1024]{1,0:T(8,128)S(1)} %get-tuple-element.146, f32[3,512]{1,0:T(4,128)S(1)} %get-tuple-element.143, f32[3,1024]{1,0:T(4,128)S(1)} %get-tuple-element.171, f32[512,1024]{1,0:T(8,128)S(1)} %get-tuple-element.147, ...), kind=kLoop, calls=%fused_computation.9.clone.1 | loop fusion | flops 12579840 | bytes 4243456 | tf_op jit(solution)/shard_map/while/body/eval_jaxpr/reduce_sum | solution.py:64
  113.3 2.4 %multiply_reduce_fusion.3 = (f32[3,512]{1,0:T(4,128)S(1)}, f32[3,512]{1,0:T(4,128)S(1)}) fusion(f32[512,1024]{1,0:T(8,128)S(1)} %get-tuple-element.146, f32[3,512]{1,0:T(4,128)S(1)} %get-tuple-element.143, f32[3,1024]{1,0:T(4,128)S(1)} %get-tuple-element.171, f32[512,1024]{1,0:T(8,128)S(1)} %get-tuple-element.147, ...), kind=kLoop, calls=%fused_computation.9.clone.1 | loop fusion | flops 12579840 | bytes 4243456 | tf_op jit(solution)/shard_map/while/body/eval_jaxpr/reduce_sum | solution.py:64
  119.0 2.4 %multiply_reduce_fusion.3 = (f32[3,512]{1,0:T(4,128)S(1)}, f32[3,512]{1,0:T(4,128)S(1)}) fusion(f32[512,1024]{1,0:T(8,128)S(1)} %get-tuple-element.146, f32[3,512]{1,0:T(4,128)S(1)} %get-tuple-element.143, f32[3,1024]{1,0:T(4,128)S(1)} %get-tuple-element.171, f32[512,1024]{1,0:T(8,128)S(1)} %get-tuple-element.147, ...), kind=kLoop, calls=%fused_computation.9.clone.1 | loop fusion | flops 12579840 | bytes 4243456 | tf_op jit(solution)/shard_map/while/body/eval_jaxpr/reduce_sum | solution.py:64
  124.2 52.9 %reduce-scatter.2.cloned.1.call-done = f32[6,256]{1,0:T(8,128)} async-done(((f32[6,4096]{1,0:T(8,128)}), f32[6,256]{1,0:T(8,128)}) %reduce-scatter.2.cloned.1.call-update) | async-done | bytes 6160 | tf_op jit(solution)/shard_map/reduce_scatter | solution.py:99
  (117 shorter events, 48.5 us)
Async XLA Ops:
  7.2 170.0 %reduce-scatter.2.cloned.1.call-start = ((), (), s32[]{:S(2)}) async-start(), calls=%async_computation.1 | async-start | bytes 139264 | tf_op jit(solution)/shard_map/reduce_scatter | solution.py:99
  12.6 8.1 %collective-permute-start = (f32[6,256]{0,1:T(8,128)S(1)}, f32[6,256]{0,1:T(8,128)S(1)}, u32[]{:S(2)}, u32[]{:S(2)}) collective-permute-start(f32[6,256]{0,1:T(8,128)S(1)} %bitcast.81), channel_id=1, source_target_pairs={{0,1},{1,2},{2,3},{3,4},{4,5},{5,6},{6,7},{7,8},{8,9},{9,10},{10,1... | collective-permute-start | bytes 18440 | tf_op jit(solution)/shard_map/ppermute | solution.py:26
  20.7 7.1 %collective-permute-start.1 = (f32[6,256]{0,1:T(8,128)S(1)}, f32[6,256]{0,1:T(8,128)S(1)}, u32[]{:S(2)}, u32[]{:S(2)}) collective-permute-start(f32[6,256]{0,1:T(8,128)S(1)} %collective-permute-done), channel_id=1, source_target_pairs={{0,1},{1,2},{2,3},{3,4},{4,5},{5,6},{6,7},{7,8},{8,9},{9,10},{10,1... | collective-permute-start | bytes 18440 | tf_op jit(solution)/shard_map/ppermute | solution.py:26
  20.7 7.1 %collective-permute-start.8 = (f32[6,256]{0,1:T(8,128)S(1)}, f32[6,256]{0,1:T(8,128)S(1)}, u32[]{:S(2)}, u32[]{:S(2)}) collective-permute-start(f32[6,256]{0,1:T(8,128)S(1)} %bitcast.82), channel_id=1, source_target_pairs={{1,0},{2,1},{3,2},{4,3},{5,4},{6,5},{7,6},{8,7},{9,8},{10,9},{11,1... | collective-permute-start | bytes 18440 | tf_op jit(solution)/shard_map/ppermute | solution.py:30
  27.8 7.2 %collective-permute-start.2 = (f32[6,256]{0,1:T(8,128)S(1)}, f32[6,256]{0,1:T(8,128)S(1)}, u32[]{:S(2)}, u32[]{:S(2)}) collective-permute-start(f32[6,256]{0,1:T(8,128)S(1)} %collective-permute-done.1), channel_id=1, source_target_pairs={{0,1},{1,2},{2,3},{3,4},{4,5},{5,6},{6,7},{7,8},{8,9},{9,10},{10,1... | collective-permute-start | bytes 18440 | tf_op jit(solution)/shard_map/ppermute | solution.py:26
  27.8 7.2 %collective-permute-start.9 = (f32[6,256]{0,1:T(8,128)S(1)}, f32[6,256]{0,1:T(8,128)S(1)}, u32[]{:S(2)}, u32[]{:S(2)}) collective-permute-start(f32[6,256]{0,1:T(8,128)S(1)} %collective-permute-done.8), channel_id=1, source_target_pairs={{1,0},{2,1},{3,2},{4,3},{5,4},{6,5},{7,6},{8,7},{9,8},{10,9},{11,1... | collective-permute-start | bytes 18440 | tf_op jit(solution)/shard_map/ppermute | solution.py:30
  35.0 7.2 %collective-permute-start.3 = (f32[6,256]{0,1:T(8,128)S(1)}, f32[6,256]{0,1:T(8,128)S(1)}, u32[]{:S(2)}, u32[]{:S(2)}) collective-permute-start(f32[6,256]{0,1:T(8,128)S(1)} %collective-permute-done.2), channel_id=1, source_target_pairs={{0,1},{1,2},{2,3},{3,4},{4,5},{5,6},{6,7},{7,8},{8,9},{9,10},{10,1... | collective-permute-start | bytes 18440 | tf_op jit(solution)/shard_map/ppermute | solution.py:26
  35.0 7.2 %collective-permute-start.10 = (f32[6,256]{0,1:T(8,128)S(1)}, f32[6,256]{0,1:T(8,128)S(1)}, u32[]{:S(2)}, u32[]{:S(2)}) collective-permute-start(f32[6,256]{0,1:T(8,128)S(1)} %collective-permute-done.9), channel_id=1, source_target_pairs={{1,0},{2,1},{3,2},{4,3},{5,4},{6,5},{7,6},{8,7},{9,8},{10,9},{11,1... | collective-permute-start | bytes 18440 | tf_op jit(solution)/shard_map/ppermute | solution.py:30
  42.2 7.2 %collective-permute-start.4 = (f32[6,256]{0,1:T(8,128)S(1)}, f32[6,256]{0,1:T(8,128)S(1)}, u32[]{:S(2)}, u32[]{:S(2)}) collective-permute-start(f32[6,256]{0,1:T(8,128)S(1)} %collective-permute-done.3), channel_id=1, source_target_pairs={{0,1},{1,2},{2,3},{3,4},{4,5},{5,6},{6,7},{7,8},{8,9},{9,10},{10,1... | collective-permute-start | bytes 18440 | tf_op jit(solution)/shard_map/ppermute | solution.py:26
  42.2 7.2 %collective-permute-start.11 = (f32[6,256]{0,1:T(8,128)S(1)}, f32[6,256]{0,1:T(8,128)S(1)}, u32[]{:S(2)}, u32[]{:S(2)}) collective-permute-start(f32[6,256]{0,1:T(8,128)S(1)} %collective-permute-done.10), channel_id=1, source_target_pairs={{1,0},{2,1},{3,2},{4,3},{5,4},{6,5},{7,6},{8,7},{9,8},{10,9},{11,1... | collective-permute-start | bytes 18440 | tf_op jit(solution)/shard_map/ppermute | solution.py:30
  49.4 7.2 %collective-permute-start.5 = (f32[6,256]{0,1:T(8,128)S(1)}, f32[6,256]{0,1:T(8,128)S(1)}, u32[]{:S(2)}, u32[]{:S(2)}) collective-permute-start(f32[6,256]{0,1:T(8,128)S(1)} %collective-permute-done.4), channel_id=1, source_target_pairs={{0,1},{1,2},{2,3},{3,4},{4,5},{5,6},{6,7},{7,8},{8,9},{9,10},{10,1... | collective-permute-start | bytes 18440 | tf_op jit(solution)/shard_map/ppermute | solution.py:26
  49.4 7.2 %collective-permute-start.12 = (f32[6,256]{0,1:T(8,128)S(1)}, f32[6,256]{0,1:T(8,128)S(1)}, u32[]{:S(2)}, u32[]{:S(2)}) collective-permute-start(f32[6,256]{0,1:T(8,128)S(1)} %collective-permute-done.11), channel_id=1, source_target_pairs={{1,0},{2,1},{3,2},{4,3},{5,4},{6,5},{7,6},{8,7},{9,8},{10,9},{11,1... | collective-permute-start | bytes 18440 | tf_op jit(solution)/shard_map/ppermute | solution.py:30
  56.6 13.1 %copy-start.6 = (f32[6,256]{0,1:T(8,128)}, f32[6,256]{0,1:T(8,128)S(1)}, u32[]{:S(2)}) copy-start(f32[6,256]{0,1:T(8,128)S(1)} %collective-permute-done.5) | copy-start | bytes 18436
  56.6 7.2 %collective-permute-start.6 = (f32[6,256]{0,1:T(8,128)S(1)}, f32[6,256]{0,1:T(8,128)S(1)}, u32[]{:S(2)}, u32[]{:S(2)}) collective-permute-start(f32[6,256]{0,1:T(8,128)S(1)} %collective-permute-done.5), channel_id=1, source_target_pairs={{0,1},{1,2},{2,3},{3,4},{4,5},{5,6},{6,7},{7,8},{8,9},{9,10},{10,1... | collective-permute-start | bytes 18440 | tf_op jit(solution)/shard_map/ppermute | solution.py:26
  56.6 13.0 %copy-start.2 = (f32[6,256]{0,1:T(8,128)}, f32[6,256]{0,1:T(8,128)S(1)}, u32[]{:S(2)}) copy-start(f32[6,256]{0,1:T(8,128)S(1)} %collective-permute-done.12) | copy-start | bytes 18436
  56.6 8.5 %collective-permute-start.13 = (f32[6,256]{0,1:T(8,128)S(1)}, f32[6,256]{0,1:T(8,128)}, u32[]{:S(2)}, u32[]{:S(2)}) collective-permute-start(f32[6,256]{0,1:T(8,128)S(1)} %collective-permute-done.12), channel_id=1, source_target_pairs={{1,0},{2,1},{3,2},{4,3},{5,4},{6,5},{7,6},{8,7},{9,8},{10,9},{11,1... | collective-permute-start | bytes 18440 | tf_op jit(solution)/shard_map/ppermute | solution.py:30
  63.8 5.9 %copy-start.7 = (f32[6,256]{0,1:T(8,128)}, f32[6,256]{0,1:T(8,128)S(1)}, u32[]{:S(2)}) copy-start(f32[6,256]{0,1:T(8,128)S(1)} %collective-permute-done.6) | copy-start | bytes 18436
  63.8 7.2 %collective-permute-start.7 = (f32[6,256]{0,1:T(8,128)S(1)}, f32[6,256]{0,1:T(8,128)}, u32[]{:S(2)}, u32[]{:S(2)}) collective-permute-start(f32[6,256]{0,1:T(8,128)S(1)} %collective-permute-done.6), channel_id=1, source_target_pairs={{0,1},{1,2},{2,3},{3,4},{4,5},{5,6},{6,7},{7,8},{8,9},{9,10},{10,1... | collective-permute-start | bytes 18440 | tf_op jit(solution)/shard_map/ppermute | solution.py:26
  65.2 9.7 %collective-permute-start.14 = (f32[6,256]{0,1:T(8,128)}, f32[6,256]{0,1:T(8,128)S(1)}, u32[]{:S(2)}, u32[]{:S(2)}) collective-permute-start(f32[6,256]{0,1:T(8,128)} %collective-permute-done.13), channel_id=1, source_target_pairs={{1,0},{2,1},{3,2},{4,3},{5,4},{6,5},{7,6},{8,7},{9,8},{10,9},{11,1... | collective-permute-start | bytes 18440 | tf_op jit(solution)/shard_map/ppermute | solution.py:30
  71.0 3.0 %copy-start.3 = (f32[6,256]{0,1:T(8,128)S(1)}, f32[6,256]{0,1:T(8,128)}, u32[]{:S(2)}) copy-start(f32[6,256]{0,1:T(8,128)} %copy-done.2) | copy-start | bytes 18436
  73.9 2.3 %copy-start.4 = (f32[8,6,512]{2,1,0:T(8,128)S(1)}, f32[8,6,512]{2,1,0:T(8,128)}, u32[]{:S(2)}) copy-start(f32[8,6,512]{2,1,0:T(8,128)} %custom-call.11) | copy-start | bytes 294916
  73.9 2.3 %copy-start.8 = (f32[1024]{0:T(1024)S(1)}, f32[1024]{0:T(1024)}, u32[]{:S(2)}) copy-start(f32[1024]{0:T(1024)} %param.11) | copy-start | bytes 12292
  76.2 46.0 %copy-start = (f32[6,1024]{1,0:T(8,128)S(1)}, f32[6,1024]{1,0:T(8,128)}, u32[]{:S(2)}) copy-start(f32[6,1024]{1,0:T(8,128)} %param.10) | copy-start | bytes 73732
  76.2 46.2 %copy-start.1 = (f32[6,1024]{1,0:T(8,128)S(1)}, f32[6,1024]{1,0:T(8,128)}, u32[]{:S(2)}) copy-start(f32[6,1024]{1,0:T(8,128)} %param.9) | copy-start | bytes 73732
  (1 other events, 0.7 us)
Sparse Core Ops, SparseCore 0:
  122.2 54.8 reduce-scatter.1
